TPU v7x, 32 devices: a whole 2x2x4 slice. The times are simulated.
32 devices in a mesh: row: 4 (over z), col: 8 (over y, x, core).
Axes of the slice: x: 2, y: 2, z: 4, core: 2. Of those that a mesh axis runs over, the one named last changes fastest.
Arguments:
- slab_left: bfloat16 [16, 8, 2048, 32], P('row', 'col'), may hold values from -6 to 6
- slab_right: bfloat16 [16, 8, 2048, 32], P('row', 'col'), may hold values from -1 to 1
- slab_ranks: int32 [16, 8], P('row', 'col'), may hold values from 20 to 32
- panel_left: bfloat16 [16, 2048, 32], P('row', 'col'), may hold values from -6 to 6
- panel_right: bfloat16 [16, 2048, 32], P('row', 'col'), may hold values from -0.125 to 0.125
- panel_ranks: int32 [16], P('row'), may hold values from 20 to 32
- inverse_factor: bfloat16 [2048, 2048], P(None, 'col'), may hold values from -2 to 2, as said below
- sketch: bfloat16 [2048, 32], replicated, may hold values from -6 to 6
Outputs:
- new_left: bfloat16 [16, 8, 2048, 32], P('row', 'col')
- new_right: bfloat16 [16, 8, 2048, 32], P('row', 'col')
Inputs may be any that keep to these rules, and one draw needn't show every extreme that they name: `slab_ranks`: number of live columns of a slab tile's factors; columns from that index on are padding. `panel_ranks`: number of live columns of a panel tile's factors; columns from that index on are padding. `inverse_factor`: lower triangular: entries above the diagonal are zero, diagonal entries positive.
All inputs are finite; a program needn't handle non-finite values.
Results may differ from a plain program's by a relative error of at most 0.0073.
Values may be sent and summed in bfloat16 or wider, within the bound.
No kernel may reach another device: no remote copies, remote signals or barrier semaphores. Data moves between devices by JAX's collectives and lax.ppermute only.
A program may use at most 64 MiB of HBM per device.

v0:
```python
import math
import jax
import jax.numpy as jnp
from jax import lax
from jax.sharding import PartitionSpec as P

highest = lax.Precision.HIGHEST
stacked_precision = lax.Precision.HIGH
shift_rate = 0.01
tiny_shift = 1e-06
factor_scale = 0.5


def spread(block, axis, owner):
    block = jnp.where(lax.axis_index(axis) == owner, block, jnp.zeros_like(block))
    return lax.psum(block, axis)


def product(first_matrix, second_matrix):
    return jnp.matmul(first_matrix, second_matrix, precision=highest)


def stacked_product(first_matrix, second_matrix):
    return jnp.matmul(first_matrix, second_matrix, precision=stacked_precision)


def flipped(matrix):
    return jnp.swapaxes(matrix, -1, -2)


def orthonormal(vectors):
    gram_matrix = product(flipped(vectors), vectors)
    shift_value = (
        shift_rate * jnp.trace(gram_matrix, axis1=-2, axis2=-1) / gram_matrix.shape[-1] + tiny_shift
    )
    identity = jnp.eye(gram_matrix.shape[-1], dtype=gram_matrix.dtype)
    lower_factor = jnp.linalg.cholesky(gram_matrix + shift_value[..., None, None] * identity)
    solved_rows = lax.linalg.triangular_solve(
        lower_factor, flipped(vectors), left_side=True, lower=True
    )
    return flipped(solved_rows)


def recompress(slab_factor, masked_right, row_factor, core_block, column_factor, sketch_float):
    target_shape = core_block.shape[:2] + slab_factor.shape[2:]
    column_wide = jnp.broadcast_to(column_factor[None], target_shape)
    row_core = product(row_factor, core_block)
    column_core = product(column_wide, flipped(core_block))
    forward_left = jnp.concatenate([slab_factor.astype(jnp.float32), -row_core], axis=-1)
    forward_right = jnp.concatenate([masked_right.astype(jnp.float32), column_wide], axis=-1)
    backward_left = jnp.concatenate([masked_right.astype(jnp.float32), -column_core], axis=-1)
    backward_right = jnp.concatenate([slab_factor.astype(jnp.float32), row_factor], axis=-1)

    def forward(vectors):
        return stacked_product(forward_left, stacked_product(flipped(forward_right), vectors))

    def backward(vectors):
        return stacked_product(backward_left, stacked_product(flipped(backward_right), vectors))

    basis_now = orthonormal(forward(sketch_float))
    basis_now = orthonormal(forward(backward(basis_now)))
    projected = backward(basis_now)
    factor_size = factor_scale * math.sqrt(slab_factor.shape[-2])
    return (basis_now * factor_size, projected / factor_size)


def shards(
    slab_left, slab_right, slab_ranks, panel_left, panel_right, panel_ranks, inverse_factor, sketch
):
    rows_total = lax.axis_size("row")
    cols_total = lax.axis_size("col")
    my_row = lax.axis_index("row")
    my_col = lax.axis_index("col")
    tile_rows, piece_rows, rank_width = panel_left.shape
    column_tiles = slab_left.shape[1]
    tile_order = inverse_factor.shape[0]
    panel_keep = jnp.arange(rank_width, dtype=jnp.int32)[None, :] < panel_ranks[:, None]
    masked_panel = jnp.where(panel_keep[:, None, :], panel_right, jnp.zeros((), jnp.bfloat16))
    flat_right = jnp.swapaxes(masked_panel, 0, 1).reshape(piece_rows, tile_rows * rank_width)
    flat_left = jnp.swapaxes(panel_left, 0, 1).reshape(piece_rows, tile_rows * rank_width)
    solved_part = lax.psum_scatter(
        jnp.dot(inverse_factor, flat_right, preferred_element_type=jnp.float32),
        "col",
        scatter_dimension=0,
        tiled=True,
    ).astype(jnp.bfloat16)
    full_left, full_solved = (
        lax.all_gather(flat_left, "col", axis=0, tiled=True),
        lax.all_gather(solved_part, "col", axis=0, tiled=True),
    )
    full_left = full_left.reshape(tile_order, tile_rows, rank_width)
    full_solved = full_solved.reshape(tile_order, tile_rows, rank_width)
    first_pick = my_col // rows_total
    position = first_pick + 0
    picked_left = lax.dynamic_slice_in_dim(full_left, position, 1, 1)
    picked_solved = lax.dynamic_slice_in_dim(full_solved, position, 1, 1)
    send_left = picked_left.reshape(tile_order, column_tiles * rank_width)
    send_solved = picked_solved.reshape(tile_order, column_tiles * rank_width)
    root_row = my_col % rows_total
    column_left, column_solved = (
        spread(send_left, "row", root_row),
        spread(send_solved, "row", root_row),
    )
    row_factor = jnp.swapaxes(full_left, 0, 1)[:, None]
    row_solved = jnp.swapaxes(full_solved, 0, 1)
    column_factor = jnp.swapaxes(column_left.reshape(tile_order, column_tiles, rank_width), 0, 1)
    column_three = jnp.swapaxes(column_solved.reshape(tile_order, column_tiles, rank_width), 0, 1)
    core_block = jnp.einsum(
        "tbr,sbq->tsrq", row_solved, column_three, preferred_element_type=jnp.float32
    )
    slab_keep = jnp.arange(rank_width, dtype=jnp.int32) < slab_ranks[..., None]
    masked_right = jnp.where(slab_keep[:, :, None, :], slab_right, jnp.zeros((), jnp.bfloat16))
    fresh_left, fresh_right = recompress(
        slab_left, masked_right, row_factor, core_block, column_factor, sketch.astype(jnp.float32)
    )
    row_ids = jnp.arange(tile_rows, dtype=jnp.int32) * rows_total + my_row
    col_ids = jnp.arange(column_tiles, dtype=jnp.int32) * cols_total + my_col
    live_tile = (row_ids[:, None] > col_ids[None, :])[:, :, None, None]
    return (
        jnp.where(live_tile, fresh_left, 0.0).astype(jnp.bfloat16),
        jnp.where(live_tile, fresh_right, 0.0).astype(jnp.bfloat16),
    )


def solution(mesh):
    placed = (
        P("row", "col", None, None),
        P("row", "col", None, None),
        P("row", "col"),
        P("row", "col", None),
        P("row", "col", None),
        P("row"),
        P(None, "col"),
        P(),
    )
    return jax.shard_map(
        shards,
        mesh=mesh,
        in_specs=placed,
        out_specs=(P("row", "col", None, None), P("row", "col", None, None)),
        check_vma=False,
    )
```

profile of v0, /device:TPU:0, one launch (start us, length us, event | category | flops | bytes accessed | tf_op | source)
XLA Modules:
  0.0 172.6 jit_solution(16440172351026109829)
XLA Ops:
  8.0 0.9 broadcast_select_fusion
  9.0 1.4 convolution_bitcast_fusion.1
  11.3 12.4 %all_gather.7 = bf16[2048,128]{0,1:T(8,128)(2,1)S(1)} all-gather(bf16[256,128]{0,1:T(8,128)(2,1)S(1)} %bitcast.193), channel_id=1, replica_groups=mesh['row'=4,'col'=8] {'col'}, dimensions={0}, use_global_device_ids=true | all-gather | bytes 589824 | tf_op jit(solution)/shard_map/all_gather | solution.py:88
  25.1 24.9 %reduce-scatter.2.cloned.1.call-done = f32[256,128]{0,1:T(8,128)} async-done(((f32[2048,128]{0,1:T(8,128)}), f32[256,128]{0,1:T(8,128)}) %reduce-scatter.2.cloned.1.call-update) | async-done | bytes 131088 | tf_op jit(solution)/shard_map/reduce_scatter | solution.py:81
  50.8 10.9 %all_gather.6 = bf16[2048,128]{0,1:T(8,128)(2,1)S(1)} all-gather(bf16[256,128]{0,1:T(8,128)(2,1)S(1)} %convert_element_type.45), channel_id=1, replica_groups=mesh['row'=4,'col'=8] {'col'}, dimensions={0}, use_global_device_ids=true | all-gather | bytes 589824 | tf_op jit(solution)/shard_map/all_gather | solution.py:89
  63.3 2.1 %convert.1 = f32[4,1,2048,32]{2,3,0,1:T(8,128)} convert(bf16[4,1,2048,32]{2,3,0,1:T(8,128)(2,1)} %bitcast.188) | non-fusion elementwise | flops 262144 | bytes 1572864 | tf_op jit(solution)/shard_map/convert_element_type | solution.py:52
  65.5 33.6 %all-reduce.3.cloned.1.call-done = (bf16[2048,32]{0,1:T(8,128)(2,1)}, bf16[2048,32]{0,1:T(8,128)(2,1)}) async-done(((bf16[2048,32]{0,1:T(8,128)(2,1)}, bf16[2048,32]{0,1:T(8,128)(2,1)}), (bf16[2048,32]{0,1:T(8,128)(2,1)}, bf16[2048,32]{0,1:T(8,128)(2,1)})) %all-reduce.3.cloned.1.call-update) | async-done | bytes 262160 | tf_op jit(solution)/shard_map/psum | solution.py:16
  99.0 1.7 fusion.38
  101.3 1.7 fusion.1
  103.1 1.0 copy-done.9
  104.1 1.1 fusion.11
  105.9 1.2 select_reduce_fusion.1
  107.4 11.9 %custom-call.8 = f32[4,1,32,32]{3,2,1,0:T(8,128)S(1)} custom-call(f32[4,1,32,32]{3,2,1,0:T(8,128)S(1)} %fusion.42), custom_call_target="Cholesky" | custom-call | tf_op jit(solution)/shard_map/jit(cholesky)/cholesky | solution.py:37
  119.5 9.8 %custom-call.9 = f32[4,1,1,32,32]{3,4,2,1,0:T(8,128)S(1)} custom-call(f32[4,1,1,32,32]{4,3,2,1,0:T(8,128)S(1)} %fusion.54), custom_call_target="InvertDiagBlocksLowerTriangular" | custom-call | tf_op jit(solution)/shard_map/triangular_solve/custom-call.0 | solution.py:38
  129.4 2.4 %convolution_bitcast_fusion = f32[4,2048,32]{1,2,0:T(8,128)S(1)} fusion(f32[4,2048,32]{1,2,0:T(8,128)} %copy-done.2, f32[4,1,1,32,32]{3,4,2,1,0:T(8,128)S(1)} %custom-call.9), kind=kOutput, calls=%fused_computation.6 | convolution fusion | flops 100663296 | bytes 2113536 | tf_op jit(solution)/shard_map/triangular_solve/dot.5 | solution.py:38
  131.8 1.0 fusion.15
  134.2 1.0 fusion.9
  136.1 1.2 select_reduce_fusion
  137.6 11.7 %custom-call.10 = f32[4,1,32,32]{3,2,1,0:T(8,128)S(1)} custom-call(f32[4,1,32,32]{3,2,1,0:T(8,128)S(1)} %fusion.40), custom_call_target="Cholesky" | custom-call | tf_op jit(solution)/shard_map/jit(cholesky)/cholesky | solution.py:37
  149.6 9.8 %custom-call.11 = f32[4,1,1,32,32]{3,4,2,1,0:T(8,128)S(1)} custom-call(f32[4,1,1,32,32]{4,3,2,1,0:T(8,128)S(1)} %fusion.49), custom_call_target="InvertDiagBlocksLowerTriangular" | custom-call | tf_op jit(solution)/shard_map/triangular_solve/custom-call.0 | solution.py:38
  159.4 2.4 %fusion.24 = f32[4,32,2048]{2,1,0:T(8,128)S(1)} fusion(f32[4,2048,32]{1,2,0:T(8,128)} %copy-done.1, f32[4,1,1,32,32]{3,4,2,1,0:T(8,128)S(1)} %custom-call.11), kind=kOutput, calls=%fused_computation.25 | convolution fusion | flops 100663296 | bytes 2113536 | tf_op jit(solution)/shard_map/triangular_solve/dot.5 | solution.py:38
  161.8 1.0 fusion.13
  162.9 1.0 fusion.34
  164.3 1.4 fusion.4
  (77 shorter events, 10.7 us)
Async XLA Ops:
  7.2 1.8 %copy-start = (bf16[2048,256]{1,0:T(8,128)(2,1)S(1)}, bf16[2048,256]{1,0:T(8,128)(2,1)}, u32[]{:S(2)}) copy-start(bf16[2048,256]{1,0:T(8,128)(2,1)} %param.17) | copy-start | bytes 3145732
  7.2 42.8 %reduce-scatter.2.cloned.1.call-start = ((), (), s32[]{:S(2)}) async-start(), calls=%async_computation.1 | async-start | bytes 1179648 | tf_op jit(solution)/shard_map/reduce_scatter | solution.py:81
  10.4 0.8 copy-start.18
  10.4 13.2 %copy-start.19 = (s32[4,1]{0,1:T(1,128)S(1)}, s32[4,1]{0,1:T(1,128)}, u32[]{:S(2)}) copy-start(s32[4,1]{0,1:T(1,128)} %param.13) | copy-start | bytes 52
  10.4 14.1 %copy-start.14 = (bf16[4,1,2048,32]{2,3,1,0:T(8,128)(2,1)S(1)}, bf16[4,1,2048,32]{2,3,1,0:T(8,128)(2,1)}, u32[]{:S(2)}) copy-start(bf16[4,1,2048,32]{2,3,1,0:T(8,128)(2,1)} %param.11) | copy-start | bytes 1572868
  10.4 88.6 %all-reduce.3.cloned.1.call-start = ((), (), s32[]{:S(2)}) async-start(), calls=%async_computation.2 | async-start | bytes 524288 | tf_op jit(solution)/shard_map/psum | solution.py:16
  23.6 0.8 copy-start.11
  23.6 1.3 copy-start.16
  61.7 0.8 copy-start.13
  99.0 1.7 copy-start.12
  99.0 2.3 %copy-start.15 = (bf16[2048,32]{0,1:T(8,128)(2,1)S(1)}, bf16[2048,32]{0,1:T(8,128)(2,1)}, u32[]{:S(2)}) copy-start(bf16[2048,32]{0,1:T(8,128)(2,1)} %get-tuple-element.8) | copy-start | bytes 393220
  101.3 3.9 %copy-start.5 = (f32[4,1,2048,32]{2,3,0,1:T(8,128)}, f32[4,1,2048,32]{2,3,0,1:T(8,128)S(1)}, u32[]{:S(2)}) copy-start(f32[4,1,2048,32]{2,3,0,1:T(8,128)S(1)} %fusion.2) | copy-start | bytes 3145732
  101.3 2.8 %copy-start.17 = (bf16[2048,32]{0,1:T(8,128)(2,1)S(1)}, bf16[2048,32]{0,1:T(8,128)(2,1)}, u32[]{:S(2)}) copy-start(bf16[2048,32]{0,1:T(8,128)(2,1)} %param.18) | copy-start | bytes 393220
  103.1 1.0 copy-start.9
  105.8 1.2 copy-start.2
  129.4 2.4 %copy-start.3 = (f32[4,1,2048,32]{2,3,0,1:T(8,128)S(1)}, f32[4,1,2048,32]{2,3,0,1:T(8,128)}, u32[]{:S(2)}) copy-start(f32[4,1,2048,32]{2,3,0,1:T(8,128)} %convert.1) | copy-start | bytes 3145732
  131.8 1.2 copy-start.7
  133.0 1.2 copy-start.10
  134.2 1.2 copy-start.6
  136.1 1.2 copy-start.1
  159.4 2.4 %copy-start.4 = (f32[4,1,2048,32]{2,3,0,1:T(8,128)S(1)}, f32[4,1,2048,32]{2,3,0,1:T(8,128)}, u32[]{:S(2)}) copy-start(f32[4,1,2048,32]{2,3,0,1:T(8,128)} %convert.1) | copy-start | bytes 3145732
  162.8 1.4 copy-start.8
Sparse Core Ops, SparseCore 0:
  11.2 38.7 reduce-scatter.1
  63.3 35.6 all-reduce.2
where the time goes:
time: 173 us
  waiting for transfers between devices  58.5 us (34%)
  other arithmetic  51.5 us (30%)
  blocking collectives  23.3 us (13%)
  matrix products  20 us (12%)
  between operations  14.4 us (8%)
  local copies, waits for them, and re-layouts  4.88 us (3%)
    psum x1, waiting for transfers between devices, spread(): return lax.psum(block, axis)  33.6 us
    reduce_scatter x1, waiting for transfers between devices, shards(): lax.psum_scatter(jnp.dot(inverse_factor, flat_right, preferred_element_ty...  24.9 us
    another operation x7, other arithmetic, orthonormal(): jnp.linalg.cholesky(gram_matrix + shift_value[..., None, None] * identity)  23.9 us
    another operation x5, other arithmetic, orthonormal(): lax.linalg.triangular_solve(lower_factor, flipped(vectors), left_side=Tru...  19.9 us
    all_gather x1, blocking collectives, shards(): lax.all_gather(flat_left, 'col', axis=0, tiled=True)  12.4 us
    all_gather x1, blocking collectives, shards(): lax.all_gather(solved_part, 'col', axis=0, tiled=True)  10.9 us
    dot_general x8, matrix products, stacked_product(): return jnp.matmul(first_matrix, second_matrix, precision=stacked_precision)  7.52 us
    another operation x2, matrix products, orthonormal(): lax.linalg.triangular_solve(lower_factor, flipped(vectors), left_side=Tru...  4.75 us
  transfers between devices with their start and end apart: 2, of which 2 were waited for; matrix products, arithmetic and copies ran while one was open for 2% of the time, Pallas kernels for 0%

commit v1 on v0

--- a/solution.py
+++ b/solution.py
@@ -13,7 +13,7 @@
 
 def spread(block, axis, owner):
     block = jnp.where(lax.axis_index(axis) == owner, block, jnp.zeros_like(block))
-    return lax.psum(block, axis)
+    return jnp.sum(lax.all_gather(block, axis), axis=0)
 
 
 def product(first_matrix, second_matrix):

time: 173 us -> 155 us (0.90)
  waiting for transfers between devices: 58.5 us -> 5.15 us
  blocking collectives: 23.3 us -> 56.2 us
  local copies, waits for them, and re-layouts: 4.88 us -> 7.38 us
    psum x1 -> x0, waiting for transfers between devices: 33.6 us -> none  [spread(): return lax.psum(block, axis)]
    all_gather x0 -> x2, blocking collectives: none -> 32.9 us  [spread(): return jnp.sum(lax.all_gather(block, axis), axis=0)]
    reduce_scatter x1, waiting for transfers between devices: 24.9 us -> 5.13 us  [shards(): lax.psum_scatter(jnp.dot(inverse_factor, flat_right, preferred_element_ty...]
    all_gather x0 -> x2, local copies, waits for them, and re-layouts: none -> 2.62 us  [spread(): return jnp.sum(lax.all_gather(block, axis), axis=0)]
    reduce_sum x0 -> x2, other arithmetic: none -> 2.36 us  [spread(): return jnp.sum(lax.all_gather(block, axis), axis=0)]
    unnamed x40 -> x38, local copies, waits for them, and re-layouts: 4.37 us -> 4.25 us
  transfers between devices with their start and end apart: 2 -> 1, of which waited for: 2 -> 1; matrix products, arithmetic and copies ran while one was open for 2% -> 2% of each run, Pallas kernels for 0% -> 0%
where the time goes in v1:
time: 155 us
  blocking collectives  56.2 us (36%)
  other arithmetic  51.6 us (33%)
  matrix products  19.9 us (13%)
  between operations  14.4 us (9%)
  local copies, waits for them, and re-layouts  7.38 us (5%)
  waiting for transfers between devices  5.15 us (3%)
    all_gather x2, blocking collectives, spread(): return jnp.sum(lax.all_gather(block, axis), axis=0)  32.9 us
    another operation x7, other arithmetic, orthonormal(): jnp.linalg.cholesky(gram_matrix + shift_value[..., None, None] * identity)  23.9 us
    another operation x5, other arithmetic, orthonormal(): lax.linalg.triangular_solve(lower_factor, flipped(vectors), left_side=Tru...  19.9 us
    all_gather x1, blocking collectives, shards(): lax.all_gather(flat_left, 'col', axis=0, tiled=True)  12.4 us
    all_gather x1, blocking collectives, shards(): lax.all_gather(solved_part, 'col', axis=0, tiled=True)  10.9 us
    dot_general x8, matrix products, stacked_product(): return jnp.matmul(first_matrix, second_matrix, precision=stacked_precision)  7.52 us
    reduce_scatter x1, waiting for transfers between devices, shards(): lax.psum_scatter(jnp.dot(inverse_factor, flat_right, preferred_element_ty...  5.13 us
    another operation x2, matrix products, orthonormal(): lax.linalg.triangular_solve(lower_factor, flipped(vectors), left_side=Tru...  4.75 us
  transfers between devices with their start and end apart: 1, of which 1 were waited for; matrix products, arithmetic and copies ran while one was open for 2% of the time, Pallas kernels for 0%

profile of v1, /device:TPU:0, one launch (start us, length us, event | category | flops | bytes accessed | tf_op | source)
XLA Modules:
  0.0 154.5 jit_solution(4203138791419071987)
XLA Ops:
  9.0 1.5 convolution_bitcast_fusion.1
  11.3 12.4 %all_gather.16 = bf16[2048,128]{0,1:T(8,128)(2,1)S(1)} all-gather(bf16[256,128]{0,1:T(8,128)(2,1)S(1)} %bitcast.193), channel_id=1, replica_groups=mesh['row'=4,'col'=8] {'col'}, dimensions={0}, use_global_device_ids=true | all-gather | bytes 589824 | tf_op jit(solution)/shard_map/all_gather | solution.py:88
  23.7 16.3 %all-gather.1 = bf16[8192,1,32]{0,2,1:T(8,128)(2,1)S(1)} all-gather(bf16[2048,1,32]{0,2,1:T(8,128)(2,1)S(1)} %dynamic-slice_select_fusion), channel_id=3, replica_groups=mesh['row'=4,'col'=8] {'row'}, dimensions={0}, use_global_device_ids=true | all-gather | bytes 655360 | tf_op jit(solution)/shard_map/all_gather | solution.py:16
  40.5 1.1 convert.3
  43.3 1.1 fusion.11
  44.8 5.1 %reduce-scatter.2.cloned.1.call-done = f32[256,128]{0,1:T(8,128)} async-done(((f32[2048,128]{0,1:T(8,128)}), f32[256,128]{0,1:T(8,128)}) %reduce-scatter.2.cloned.1.call-update) | async-done | bytes 131088 | tf_op jit(solution)/shard_map/reduce_scatter | solution.py:81
  50.8 10.9 %all_gather.14 = bf16[2048,128]{0,1:T(8,128)(2,1)S(1)} all-gather(bf16[256,128]{0,1:T(8,128)(2,1)S(1)} %convert_element_type.51), channel_id=1, replica_groups=mesh['row'=4,'col'=8] {'col'}, dimensions={0}, use_global_device_ids=true | all-gather | bytes 589824 | tf_op jit(solution)/shard_map/all_gather | solution.py:89
  62.5 16.6 %all-gather = bf16[8192,1,32]{0,2,1:T(8,128)(2,1)} all-gather(bf16[2048,1,32]{0,2,1:T(8,128)(2,1)S(1)} %dynamic-slice_select_fusion.1), channel_id=2, replica_groups=mesh['row'=4,'col'=8] {'row'}, dimensions={0}, use_global_device_ids=true | all-gather | bytes 655360 | tf_op jit(solution)/shard_map/all_gather | solution.py:16
  79.1 2.2 %reshape.197 = bf16[4,2048,32]{1,0,2:T(4,128)(2,1)} reshape(bf16[8192,1,32]{0,2,1:T(8,128)(2,1)} %all-gather) | data formatting | bytes 1048576 | tf_op jit(solution)/shard_map/all_gather | solution.py:16
  81.4 1.7 %reduce_sum.40 = bf16[2048,32]{0,1:T(8,128)(2,1)S(1)} reduce(bf16[4,2048,32]{1,0,2:T(4,128)(2,1)} %reshape.197, bf16[]{:T(256)} %constant.85.clone.1), dimensions={0}, to_apply=%region_1.2 | reduce | flops 196608 | bytes 655362 | tf_op jit(solution)/shard_map/reduce_sum | solution.py:16
  83.1 1.6 %fusion.38 = f32[32,4,32]{2,0,1:T(8,128)S(1)} fusion(bf16[4,2048,32]{1,2,0:T(8,128)(2,1)} %bitcast.191, bf16[2048,32]{0,1:T(8,128)(2,1)S(1)} %reduce_sum.40), kind=kOutput, calls=%fused_computation.42 | convolution fusion | flops 16777216 | bytes 671744 | tf_op jit(solution)/shard_map/tbr,sbq->tsrq/dot_general | solution.py:108
  84.7 1.6 %fusion.1 = f32[4,1,2048,32]{2,3,0,1:T(8,128)} fusion(bf16[2048,32]{0,1:T(8,128)(2,1)S(1)} %reduce_sum.41, f32[32,4,32]{2,0,1:T(8,128)S(1)} %fusion.38), kind=kOutput, calls=%fused_computation.8 | convolution fusion | flops 100925440 | bytes 1196032 | tf_op jit(solution)/shard_map/dot_general | solution.py:20
  87.8 1.2 select_reduce_fusion.1
  89.4 11.9 %custom-call.8 = f32[4,1,32,32]{3,2,1,0:T(8,128)S(1)} custom-call(f32[4,1,32,32]{3,2,1,0:T(8,128)S(1)} %fusion.42), custom_call_target="Cholesky" | custom-call | tf_op jit(solution)/shard_map/jit(cholesky)/cholesky | solution.py:37
  101.5 9.8 %custom-call.9 = f32[4,1,1,32,32]{3,4,2,1,0:T(8,128)S(1)} custom-call(f32[4,1,1,32,32]{4,3,2,1,0:T(8,128)S(1)} %fusion.54), custom_call_target="InvertDiagBlocksLowerTriangular" | custom-call | tf_op jit(solution)/shard_map/triangular_solve/custom-call.0 | solution.py:38
  111.4 2.4 %convolution_bitcast_fusion = f32[4,2048,32]{1,2,0:T(8,128)S(1)} fusion(f32[4,2048,32]{1,2,0:T(8,128)} %copy-done.2, f32[4,1,1,32,32]{3,4,2,1,0:T(8,128)S(1)} %custom-call.9), kind=kOutput, calls=%fused_computation.6 | convolution fusion | flops 100663296 | bytes 2113536 | tf_op jit(solution)/shard_map/triangular_solve/dot.5 | solution.py:38
  113.8 1.0 fusion.15
  116.2 1.0 fusion.9
  118.1 1.2 select_reduce_fusion
  119.6 11.7 %custom-call.10 = f32[4,1,32,32]{3,2,1,0:T(8,128)S(1)} custom-call(f32[4,1,32,32]{3,2,1,0:T(8,128)S(1)} %fusion.40), custom_call_target="Cholesky" | custom-call | tf_op jit(solution)/shard_map/jit(cholesky)/cholesky | solution.py:37
  131.6 9.8 %custom-call.11 = f32[4,1,1,32,32]{3,4,2,1,0:T(8,128)S(1)} custom-call(f32[4,1,1,32,32]{4,3,2,1,0:T(8,128)S(1)} %fusion.49), custom_call_target="InvertDiagBlocksLowerTriangular" | custom-call | tf_op jit(solution)/shard_map/triangular_solve/custom-call.0 | solution.py:38
  141.4 2.4 %fusion.24 = f32[4,32,2048]{2,1,0:T(8,128)S(1)} fusion(f32[4,2048,32]{1,2,0:T(8,128)} %copy-done.1, f32[4,1,1,32,32]{3,4,2,1,0:T(8,128)S(1)} %custom-call.11), kind=kOutput, calls=%fused_computation.25 | convolution fusion | flops 100663296 | bytes 2113536 | tf_op jit(solution)/shard_map/triangular_solve/dot.5 | solution.py:38
  143.8 1.0 fusion.13
  146.2 1.4 fusion.4
  (78 shorter events, 13.2 us)
Async XLA Ops:
  7.2 1.8 %copy-start = (bf16[2048,256]{1,0:T(8,128)(2,1)S(1)}, bf16[2048,256]{1,0:T(8,128)(2,1)}, u32[]{:S(2)}) copy-start(bf16[2048,256]{1,0:T(8,128)(2,1)} %param.17) | copy-start | bytes 3145732
  7.2 42.8 %reduce-scatter.2.cloned.1.call-start = ((), (), s32[]{:S(2)}) async-start(), calls=%async_computation.1 | async-start | bytes 1179648 | tf_op jit(solution)/shard_map/reduce_scatter | solution.py:81
  10.4 0.8 copy-start.17
  23.7 18.0 %copy-start.11 = (bf16[2048,128]{0,1:T(8,128)(2,1)}, bf16[2048,128]{0,1:T(8,128)(2,1)S(1)}, u32[]{:S(2)}) copy-start(bf16[2048,128]{0,1:T(8,128)(2,1)S(1)} %all_gather.16) | copy-start | bytes 1572868
  40.5 1.8 %copy-start.18 = (s32[4,1]{0,1:T(1,128)S(1)}, s32[4,1]{0,1:T(1,128)}, u32[]{:S(2)}) copy-start(s32[4,1]{0,1:T(1,128)} %param.13) | copy-start | bytes 52
  40.5 1.9 %copy-start.15 = (bf16[4,1,2048,32]{2,3,1,0:T(8,128)(2,1)S(1)}, bf16[4,1,2048,32]{2,3,1,0:T(8,128)(2,1)}, u32[]{:S(2)}) copy-start(bf16[4,1,2048,32]{2,3,1,0:T(8,128)(2,1)} %param.12) | copy-start | bytes 1572868
  42.4 0.9 copy-start.16
  43.3 1.1 copy-start.9
  43.3 1.4 copy-start.14
  61.7 0.8 copy-start.13
  83.0 3.2 %copy-start.12 = (bf16[2048,128]{0,1:T(8,128)(2,1)S(1)}, bf16[2048,128]{0,1:T(8,128)(2,1)}, u32[]{:S(2)}) copy-start(bf16[2048,128]{0,1:T(8,128)(2,1)} %copy-done.11) | copy-start | bytes 1572868
  86.8 1.0 copy-start.5
  87.8 1.2 copy-start.2
  111.4 2.4 %copy-start.3 = (f32[4,1,2048,32]{2,3,0,1:T(8,128)S(1)}, f32[4,1,2048,32]{2,3,0,1:T(8,128)}, u32[]{:S(2)}) copy-start(f32[4,1,2048,32]{2,3,0,1:T(8,128)} %convert.3) | copy-start | bytes 3145732
  113.7 1.2 copy-start.7
  115.0 1.2 copy-start.10
  116.2 1.2 copy-start.6
  118.1 1.2 copy-start.1
  141.4 2.4 %copy-start.4 = (f32[4,1,2048,32]{2,3,0,1:T(8,128)S(1)}, f32[4,1,2048,32]{2,3,0,1:T(8,128)}, u32[]{:S(2)}) copy-start(f32[4,1,2048,32]{2,3,0,1:T(8,128)} %convert.3) | copy-start | bytes 3145732
  144.8 1.4 copy-start.8
Sparse Core Ops, SparseCore 0:
  11.2 38.7 reduce-scatter.1
